TPU v7x, 256 devices: a whole 4x4x8 slice. The times are simulated.
256 devices in a mesh: chan: 8 (over y_hi, x), win: 32 (over y_lo, z, core).
Axes of the slice: x: 4, y: 4 (y_hi: 2, y_lo: 2; y = y_hi * 2 + y_lo), z: 8, core: 2. Of those that a mesh axis runs over, the one named last changes fastest.
Arguments:
- raw: bfloat16 [128, 3200, 1024], P('win', None, 'chan'), may hold values from -6 to 6
- offsets: int32 [128], P('win'), may hold values from 0 to 128
- quality: int32 [128, 1024], P('win', 'chan'), may hold values 0 or 1
Outputs:
- stack: bfloat16 [384, 2, 1024, 1024], P('win', None, 'chan')
All inputs are finite; a program needn't handle non-finite values. No bound on the sum of `quality` on one device may be relied on, other than what follows from the above.
Results may differ from a plain program's by a relative error of at most 0.0064.
Values may be sent and summed in bfloat16 or wider, within the bound.
A program may use at most 64 MiB of HBM per device.

v0:
```python
import math
import jax
import jax.numpy as jnp
from jax import lax
from jax.sharding import PartitionSpec as P

F = 384
L = 3072
FIRST_BIN = 60
epsilon = 1e-05


def dft_table():
    sample_idx = jnp.arange(L, dtype=jnp.int32)
    bin_idx = FIRST_BIN + jnp.arange(F, dtype=jnp.int32)
    residue = bin_idx[:, None] * sample_idx[None, :] % L
    angles = residue.astype(jnp.float32) * (2.0 * math.pi / L)
    return jnp.concatenate([jnp.cos(angles), -jnp.sin(angles)], 0).astype(jnp.bfloat16)


def cross_spectra(mine, partner):
    stack_scale = 1.0 / math.sqrt(mine.shape[0])
    real_mine = mine[:, 0]
    imag_mine = mine[:, 1]
    real_other = partner[:, 0]
    imag_other = partner[:, 1]
    real_part = jnp.einsum(
        "wfi,wfj->fij", real_mine, real_other, preferred_element_type=jnp.float32
    )
    real_part = real_part + jnp.einsum(
        "wfi,wfj->fij", imag_mine, imag_other, preferred_element_type=jnp.float32
    )
    imag_part = jnp.einsum(
        "wfi,wfj->fij", imag_mine, real_other, preferred_element_type=jnp.float32
    )
    imag_part = imag_part - jnp.einsum(
        "wfi,wfj->fij", real_mine, imag_other, preferred_element_type=jnp.float32
    )
    return (jnp.stack([real_part, imag_part], 1) * stack_scale).astype(jnp.bfloat16)


def local(raw, offsets, quality):
    table = dft_table()

    def cut_window(segment, shift_at):
        return lax.dynamic_slice_in_dim(segment, shift_at, L, 0)

    windows = jax.vmap(cut_window)(raw, offsets)
    transform = jnp.einsum("kl,wlc->wkc", table, windows, preferred_element_type=jnp.float32)
    band_power = jnp.sum(transform * transform, axis=1, keepdims=True) / F
    whiten = lax.rsqrt(band_power + epsilon) * quality.astype(jnp.float32)[:, None, :]
    block_width = raw.shape[2]
    spectra = (transform * whiten).astype(jnp.bfloat16).reshape(raw.shape[0], 2, F, block_width)
    gathered = lax.all_gather(spectra, "chan", axis=3, tiled=True)
    by_bin = lax.all_to_all(gathered, "win", split_axis=2, concat_axis=0, tiled=True)
    mine = lax.dynamic_slice_in_dim(by_bin, lax.axis_index("chan") * block_width, block_width, 3)
    return cross_spectra(mine, by_bin)


def solution(mesh):
    in_specs = (P("win", None, "chan"), P("win"), P("win", "chan"))
    out_specs = P("win", None, "chan", None)
    return jax.shard_map(local, mesh=mesh, in_specs=in_specs, out_specs=out_specs, check_vma=False)
```

profile of v0, /device:TPU:96, one launch (start us, length us, event | category | flops | bytes accessed | tf_op | source)
XLA Modules:
  0.0 393.1 jit_solution(9089974725493236142)
XLA Ops:
  6.5 0.0 all-gather.2.cloned.1.call-start
  6.5 0.7 fusion.14
  7.2 0.1 copy.21
  7.3 13.5 %while.1 = (s32[]{:T(128)}, bf16[4,3200,128]{2,1,0:T(8,128)(2,1)}, s32[4,3]{1,0:T(4,128)S(1)}, bf16[4,3072,128]{2,1,0:T(8,128)(2,1)S(1)}, s32[]{:T(128)}) while((s32[]{:T(128)}, bf16[4,3200,128]{2,1,0:T(8,128)(2,1)}, s32[4,3]{1,0:T(4,128)S(1)}, bf16[4,3072,128]{2,1,0:T(8,128)(2,1)S(1)}, s32[]{:T(128)}) %tuple.24), condition=%wide.while_cond, body=%wide.while_body.sunk | while | flops 2 | bytes 1572989 | solution.py:46
  7.3 0.7 fusion.23
  8.0 2.7 dynamic-slice_dynamic-update-slice_fusion.2
  10.7 0.7 fusion.23
  11.4 2.7 dynamic-slice_dynamic-update-slice_fusion.2
  14.1 0.7 fusion.23
  14.7 2.7 dynamic-slice_dynamic-update-slice_fusion.2
  17.5 0.7 fusion.23
  18.1 2.7 dynamic-slice_dynamic-update-slice_fusion.2
  20.8 20.3 %cosine_convert_fusion = (bf16[384,3072]{1,0:T(8,128)(2,1)S(1)}, bf16[384,3072]{1,0:T(8,128)(2,1)S(1)}) fusion(s32[384]{0:T(512)S(1)} %iota_add_fusion), kind=kLoop, calls=%fused_computation.14 | loop fusion | flops 14155776 | bytes 4720128 | tf_op jit(solution)/shard_map/convert
  41.1 0.0 copy-start.1
  41.1 2.8 multiply_reduce_fusion
  43.9 0.0 copy-done.1
  43.9 0.2 fusion.13
  44.1 0.2 reshape.12
  44.3 2.1 copy.23
  46.3 0.0 all-gather.2.cloned.1.call-update
  46.4 159.5 %all-gather.2.cloned.1.call-done = bf16[4,2,384,1024]{3,1,0,2:T(2,128)(2,1)} async-done(((bf16[4,2,384,128]{3,1,0,2:T(2,128)(2,1)}), bf16[4,2,384,1024]{3,1,0,2:T(2,128)(2,1)}) %all-gather.2.cloned.1.call-update) | async-done | bytes 6291472 | tf_op jit(solution)/shard_map/all_gather | solution.py:54
  205.9 7.5 %all-to-all-start = ((bf16[4,2,384,1024]{3,1,0,2:T(2,128)(2,1)}), bf16[4,2,384,1024]{3,1,0,2:T(2,128)(2,1)}, u32[]{:S(2)}, u32[]{:S(2)}) async-start(bf16[4,2,384,1024]{3,1,0,2:T(2,128)(2,1)} %all-gather.2.cloned.1.call-done), calls=%async_computation | async-start | bytes 12582912 | tf_op jit(solution)/shard_map/all_to_all | solution.py:55
  213.4 142.0 %all-to-all-done = bf16[4,2,384,1024]{3,1,0,2:T(2,128)(2,1)} async-done(((bf16[4,2,384,1024]{3,1,0,2:T(2,128)(2,1)}), bf16[4,2,384,1024]{3,1,0,2:T(2,128)(2,1)}, u32[]{:S(2)}, u32[]{:S(2)}) %all-to-all-start) | async-done | bytes 6291488 | tf_op jit(solution)/shard_map/all_to_all | solution.py:55
  355.4 8.8 %copy.25 = bf16[32,4,2,12,1024]{4,1,0,3,2:T(4,128)(2,1)} copy(bf16[32,4,2,12,1024]{4,2,1,3,0:T(2,128)(2,1)} %bitcast.5) | data formatting | bytes 12582912 | tf_op jit(solution)/shard_map/all_to_all | solution.py:55
  364.1 9.7 %all_to_all.16 = bf16[128,2,12,1024]{3,0,2,1:T(8,128)(2,1)} reshape(bf16[32,4,2,12,1024]{4,1,0,3,2:T(4,128)(2,1)} %copy.25) | data formatting | bytes 12582912 | tf_op jit(solution)/shard_map/all_to_all | solution.py:55
  373.8 0.0 copy-start
  373.8 3.2 fusion.10
  377.0 0.7 copy-done
  377.7 1.0 fusion.9
  378.7 1.0 add_bitcast_fusion
  379.8 1.0 subtract_bitcast_fusion
  380.8 1.9 fusion
  382.8 3.5 copy.30
  (9 shorter events, 0.1 us)
Async XLA Ops:
  6.5 199.3 %all-gather.2.cloned.1.call-start = ((), (), s32[]{:S(2)}) async-start(), calls=%async_computation.1 | async-start | bytes 7077888 | tf_op jit(solution)/shard_map/all_gather | solution.py:54
  41.1 2.8 copy-start.1
  205.9 149.5 %all-to-all-start = ((bf16[4,2,384,1024]{3,1,0,2:T(2,128)(2,1)}), bf16[4,2,384,1024]{3,1,0,2:T(2,128)(2,1)}, u32[]{:S(2)}, u32[]{:S(2)}) async-start(bf16[4,2,384,1024]{3,1,0,2:T(2,128)(2,1)} %all-gather.2.cloned.1.call-done), calls=%async_computation | async-start | bytes 12582912 | tf_op jit(solution)/shard_map/all_to_all | solution.py:55
  373.8 3.9 copy-start
Sparse Core Ops, SparseCore 0:
  46.5 159.3 all-gather.1
where the time goes:
time: 394 us; the launch traced here: 393 us
  waiting for transfers between devices  301 us (76%)
  local copies, waits for them, and re-layouts  38.4 us (10%)
  other arithmetic  23 us (6%)
  between operations  13.5 us (3%)
  matrix products  9.09 us (2%)
  starting transfers between devices  7.54 us (2%)
    all_gather x1, waiting for transfers between devices, local(): gathered = lax.all_gather(spectra, 'chan', axis=3, tiled=True)  159 us
    all_to_all x1, waiting for transfers between devices, local(): lax.all_to_all(gathered, 'win', split_axis=2, concat_axis=0, tiled=True)  142 us
    another operation x1, other arithmetic  20.3 us
    all_to_all x2, local copies, waits for them, and re-layouts, local(): lax.all_to_all(gathered, 'win', split_axis=2, concat_axis=0, tiled=True)  18.4 us
    gather x12, local copies, waits for them, and re-layouts  13.4 us
  transfers between devices with their start and end apart: 2, of which 2 were waited for; matrix products, arithmetic and copies ran while one was open for 0% of the time, Pallas kernels for 0%

commit v1 on v0

--- a/solution.py
+++ b/solution.py
@@ -51,7 +51,10 @@
     whiten = lax.rsqrt(band_power + epsilon) * quality.astype(jnp.float32)[:, None, :]
     block_width = raw.shape[2]
     spectra = (transform * whiten).astype(jnp.bfloat16).reshape(raw.shape[0], 2, F, block_width)
-    gathered = lax.all_gather(spectra, "chan", axis=3, tiled=True)
+    n_dev = lax.axis_size("chan")
+    blocks = jnp.stack([spectra for _ in range(n_dev)])
+    blocks = lax.all_to_all(blocks, "chan", split_axis=0, concat_axis=0)
+    gathered = jnp.concatenate(blocks, axis=3)
     by_bin = lax.all_to_all(gathered, "win", split_axis=2, concat_axis=0, tiled=True)
     mine = lax.dynamic_slice_in_dim(by_bin, lax.axis_index("chan") * block_width, block_width, 3)
     return cross_spectra(mine, by_bin)

time: 394 us -> 321 us (0.81)
  waiting for transfers between devices: 301 us -> 142 us
  blocking collectives: 0 us -> 80.7 us
  local copies, waits for them, and re-layouts: 38.4 us -> 56.5 us
  between operations: 13.5 us -> 0.11 us
    all_gather x1 -> x0, waiting for transfers between devices: 159 us -> none  [local(): gathered = lax.all_gather(spectra, 'chan', axis=3, tiled=True)]
    all_to_all x0 -> x1, blocking collectives: none -> 80.7 us  [local(): blocks = lax.all_to_all(blocks, 'chan', split_axis=0, concat_axis=0)]
    reshape x2 -> x1, local copies, waits for them, and re-layouts: 2.27 us -> 16.2 us  [local(): gathered = jnp.concatenate(blocks, axis=3)]
  transfers between devices with their start and end apart: 2 -> 1, of which waited for: 2 -> 1; matrix products, arithmetic and copies ran while one was open for 0% -> 0% of each run, Pallas kernels for 0% -> 0%
where the time goes in v1:
time: 321 us; the launch traced here: 319 us
  waiting for transfers between devices  142 us (44%)
  blocking collectives  80.7 us (25%)
  local copies, waits for them, and re-layouts  56.5 us (18%)
  other arithmetic  23 us (7%)
  matrix products  9.09 us (3%)
  starting transfers between devices  7.99 us (2%)
    all_to_all x1, waiting for transfers between devices, local(): lax.all_to_all(gathered, 'win', split_axis=2, concat_axis=0, tiled=True)  142 us
    all_to_all x1, blocking collectives, local(): blocks = lax.all_to_all(blocks, 'chan', split_axis=0, concat_axis=0)  80.7 us
    another operation x1, other arithmetic  20.3 us
    all_to_all x2, local copies, waits for them, and re-layouts, local(): lax.all_to_all(gathered, 'win', split_axis=2, concat_axis=0, tiled=True)  18.4 us
    reshape x1, local copies, waits for them, and re-layouts, local(): gathered = jnp.concatenate(blocks, axis=3)  16.2 us
    gather x12, local copies, waits for them, and re-layouts  13 us
    all_to_all x1, starting transfers between devices, local(): lax.all_to_all(gathered, 'win', split_axis=2, concat_axis=0, tiled=True)  7.99 us
  transfers between devices with their start and end apart: 1, of which 1 were waited for; matrix products, arithmetic and copies ran while one was open for 0% of the time, Pallas kernels for 0%

profile of v1, /device:TPU:96, one launch (start us, length us, event | category | flops | bytes accessed | tf_op | source)
XLA Modules:
  0.0 319.4 jit_solution(11465223586393775873)
XLA Ops:
  0.0 0.7 fusion.13
  0.7 0.1 copy.22
  0.8 13.0 %while.1 = (s32[]{:T(128)}, bf16[4,3200,128]{2,1,0:T(8,128)(2,1)}, s32[4,3]{1,0:T(4,128)S(1)}, bf16[4,3072,128]{2,1,0:T(8,128)(2,1)S(1)}, s32[]{:T(128)}) while((s32[]{:T(128)}, bf16[4,3200,128]{2,1,0:T(8,128)(2,1)}, s32[4,3]{1,0:T(4,128)S(1)}, bf16[4,3072,128]{2,1,0:T(8,128)(2,1)S(1)}, s32[]{:T(128)}) %tuple.24), condition=%wide.while_cond, body=%wide.while_body.sunk | while | flops 2 | bytes 1572989 | solution.py:46
  0.8 0.6 fusion.22
  1.4 2.6 dynamic-slice_dynamic-update-slice_fusion.2
  4.0 0.6 fusion.22
  4.6 2.6 dynamic-slice_dynamic-update-slice_fusion.2
  7.3 0.6 fusion.22
  7.9 2.6 dynamic-slice_dynamic-update-slice_fusion.2
  10.6 0.6 fusion.22
  11.2 2.6 dynamic-slice_dynamic-update-slice_fusion.2
  13.8 20.3 %cosine_convert_fusion = (bf16[384,3072]{1,0:T(8,128)(2,1)S(1)}, bf16[384,3072]{1,0:T(8,128)(2,1)S(1)}) fusion(s32[384]{0:T(512)S(1)} %iota_add_fusion), kind=kLoop, calls=%fused_computation.14 | loop fusion | flops 14155776 | bytes 4720128 | tf_op jit(solution)/shard_map/convert
  34.1 0.0 copy-start.1
  34.1 2.8 multiply_reduce_fusion
  36.9 0.0 copy-done.1
  36.9 0.2 multiply_convert_fusion
  37.1 0.1 copy.42
  37.2 1.0 stack.12
  38.2 80.7 %all_to_all.23 = bf16[8,4,2,384,128]{3,4,2,1,0:T(8,128)(2,1)S(1)} all-to-all(bf16[8,4,2,384,128]{3,4,2,1,0:T(8,128)(2,1)S(1)} %stack.12), channel_id=1, replica_groups=mesh['chan'=8,'win'=32] {'chan'}, dimensions={0} | all-to-all | bytes 12582912 | tf_op jit(solution)/shard_map/all_to_all | solution.py:56
  118.8 3.6 %copy.25 = bf16[8,4,2,384,128]{3,4,0,2,1:T(8,128)(2,1)} copy(bf16[8,4,2,384,128]{3,4,2,1,0:T(8,128)(2,1)S(1)} %all_to_all.23) | data formatting | bytes 12582912 | tf_op jit(solution)/shard_map/all_to_all | solution.py:56
  122.4 16.2 %copy.26 = bf16[4,2,384,1024]{3,1,0,2:T(2,128)(2,1)} copy(bf16[4,2,384,1024]{2,3,1,0:T(8,128)(2,1)} %bitcast.51) | data formatting | bytes 12582912 | tf_op jit(solution)/shard_map/reshape | solution.py:57
  138.6 8.0 %all-to-all-start.1 = ((bf16[4,2,384,1024]{3,1,0,2:T(2,128)(2,1)}), bf16[4,2,384,1024]{3,1,0,2:T(2,128)(2,1)}, u32[]{:S(2)}, u32[]{:S(2)}) async-start(bf16[4,2,384,1024]{3,1,0,2:T(2,128)(2,1)} %copy.26), calls=%async_computation.1 | async-start | bytes 12582912 | tf_op jit(solution)/shard_map/all_to_all | solution.py:58
  146.6 142.0 %all-to-all-done.1 = bf16[4,2,384,1024]{3,1,0,2:T(2,128)(2,1)} async-done(((bf16[4,2,384,1024]{3,1,0,2:T(2,128)(2,1)}), bf16[4,2,384,1024]{3,1,0,2:T(2,128)(2,1)}, u32[]{:S(2)}, u32[]{:S(2)}) %all-to-all-start.1) | async-done | bytes 6291488 | tf_op jit(solution)/shard_map/all_to_all | solution.py:58
  288.6 8.8 %copy.28 = bf16[32,4,2,12,1024]{4,1,0,3,2:T(4,128)(2,1)} copy(bf16[32,4,2,12,1024]{4,2,1,3,0:T(2,128)(2,1)} %bitcast.7) | data formatting | bytes 12582912 | tf_op jit(solution)/shard_map/all_to_all | solution.py:58
  297.3 9.7 %all_to_all.20 = bf16[128,2,12,1024]{3,0,2,1:T(8,128)(2,1)} reshape(bf16[32,4,2,12,1024]{4,1,0,3,2:T(4,128)(2,1)} %copy.28) | data formatting | bytes 12582912 | tf_op jit(solution)/shard_map/all_to_all | solution.py:58
  307.0 0.0 copy-start
  307.0 3.2 fusion.10
  310.2 0.7 copy-done
  310.9 1.0 fusion.9
  311.9 1.0 add_bitcast_fusion
  312.9 1.0 subtract_bitcast_fusion
  314.0 1.9 fusion
  315.9 3.5 %copy.33 = bf16[12,2,128,1024]{3,2,1,0:T(8,128)(2,1)} copy(bf16[12,2,128,1024]{3,2,0,1:T(8,128)(2,1)S(1)} %fusion) | data formatting | bytes 12582912 | tf_op jit(solution)/shard_map/convert_element_type | solution.py:39
  (9 shorter events, 0.1 us)
Async XLA Ops:
  34.1 2.8 copy-start.1
  138.6 150.0 %all-to-all-start.1 = ((bf16[4,2,384,1024]{3,1,0,2:T(2,128)(2,1)}), bf16[4,2,384,1024]{3,1,0,2:T(2,128)(2,1)}, u32[]{:S(2)}, u32[]{:S(2)}) async-start(bf16[4,2,384,1024]{3,1,0,2:T(2,128)(2,1)} %copy.26), calls=%async_computation.1 | async-start | bytes 12582912 | tf_op jit(solution)/shard_map/all_to_all | solution.py:58
  307.0 3.9 %copy-start = (bf16[128,2,12,1024]{3,0,2,1:T(8,128)(2,1)S(1)}, bf16[128,2,12,1024]{3,0,2,1:T(8,128)(2,1)}, u32[]{:S(2)}) copy-start(bf16[128,2,12,1024]{3,0,2,1:T(8,128)(2,1)} %all_to_all.20) | copy-start | bytes 18874372
